TPU v7x, 32 devices: a whole 2x2x4 slice. The times are simulated.
32 devices in a mesh: rows: 4 (over x, core), cols: 8 (over z, y).
Axes of the slice: x: 2, y: 2, z: 4, core: 2. Of those that a mesh axis runs over, the one named last changes fastest.
Arguments:
- tensor: float32 [48, 256, 512], P('rows', 'cols'), may hold values from 0 to 1
- first_factor: float32 [48, 256], P('rows', 'cols'), may hold values from -2.5 to 2.5
- second_factor: float32 [256, 256], P('cols', 'rows'), may hold values from -2.5 to 2.5
- third_factor: float32 [512, 256], P(('rows', 'cols')), may hold values from -2.5 to 2.5
Outputs:
- first_new: float32 [48, 256], P('rows', 'cols')
- second_new: float32 [256, 256], P('cols', 'rows')
- third_new: float32 [512, 256], P(('rows', 'cols'))
All inputs are finite; a program needn't handle non-finite values.
Results may differ from a plain program's by a relative error of at most 0.0003.
Values sent between devices are 32-bit elements; how exact they have to be, the bound alone decides.
A program may use at most 64 MiB of HBM per device.

v0:
```python
import jax
import jax.numpy as jnp
from jax import lax
from jax.sharding import PartitionSpec as P

STEPS = 2


def gather_third(piece):
    return lax.all_gather(piece, ("rows", "cols"), axis=0, tiled=True)


def per_device(tensor, first_factor, second_factor, third_factor):
    high = lax.Precision.HIGHEST
    rows_dev, cols_dev, depth = tensor.shape
    size_i = rows_dev * lax.axis_size("rows")
    size_j = cols_dev * lax.axis_size("cols")
    rate_a = 4.0 / jnp.sqrt(jnp.float32(size_j * depth))
    rate_b = 4.0 / jnp.sqrt(jnp.float32(size_i * depth))
    rate_c = 4.0 / jnp.sqrt(jnp.float32(size_i * size_j))
    flat_target = tensor.reshape(-1, depth)
    shard_a, shard_b = (first_factor, second_factor)
    whole_c = gather_third(third_factor)
    for step_index in range(STEPS):
        whole_a = lax.all_gather(shard_a, "cols", axis=1, tiled=True)
        whole_b = lax.all_gather(shard_b, "rows", axis=1, tiled=True)
        khatri = (whole_a[:, None, :] * whole_b[None, :, :]).reshape(-1, whole_a.shape[1])
        model_tile = jnp.dot(khatri, whole_c.T, precision=high, preferred_element_type=jnp.float32)
        deriv = jax.nn.sigmoid(model_tile) - flat_target
        deriv_c = jnp.dot(
            deriv, whole_c, precision=high, preferred_element_type=jnp.float32
        ).reshape(rows_dev, cols_dev, -1)
        term_a = jnp.einsum("ijr,jr->ir", deriv_c, whole_b, precision=high)
        term_b = jnp.einsum("ijr,ir->jr", deriv_c, whole_a, precision=high)
        term_c = lax.dot_general(
            deriv,
            khatri,
            (((0,), (0,)), ((), ())),
            precision=high,
            preferred_element_type=jnp.float32,
        )
        shard_a = shard_a - rate_a * lax.psum_scatter(
            term_a, "cols", scatter_dimension=1, tiled=True
        )
        shard_b = shard_b - rate_b * lax.psum_scatter(
            term_b, "rows", scatter_dimension=1, tiled=True
        )
        whole_c = whole_c - rate_c * lax.psum(term_c, ("rows", "cols"))
    owner = lax.axis_index("rows") * lax.axis_size("cols") + lax.axis_index("cols")
    count = third_factor.shape[0]
    shard_c = lax.dynamic_slice_in_dim(whole_c, owner * count, count, 0)
    return (shard_a, shard_b, shard_c)


def solution(mesh):
    in_specs = (
        P("rows", "cols", None),
        P("rows", "cols"),
        P("cols", "rows"),
        P(("rows", "cols"), None),
    )
    out_specs = (P("rows", "cols"), P("cols", "rows"), P(("rows", "cols"), None))
    return jax.shard_map(
        per_device, mesh=mesh, in_specs=in_specs, out_specs=out_specs, check_vma=False
    )
```

profile of v0, /device:TPU:0, one launch (start us, length us, event | category | flops | bytes accessed | tf_op | source)
XLA Modules:
  0.0 396.7 jit_solution(13207134595895252881)
XLA Ops:
  8.0 6.5 %all-gather.1 = f32[4,64,32]{1,2,0:T(8,128)S(1)} all-gather(f32[1,64,32]{1,2,0:T(8,128)} %bitcast.87), channel_id=1, replica_groups=mesh['rows'=4,'cols'=8] {'rows'}, dimensions={0}, use_global_device_ids=true | all-gather | bytes 40960 | tf_op jit(solution)/shard_map/all_gather | solution.py:26
  15.2 31.3 %all-gather = f32[8,32,12]{1,2,0:T(8,128)S(1)} all-gather(f32[1,32,12]{1,2,0:T(8,128)S(1)} %bitcast.90), channel_id=1, replica_groups=mesh['rows'=4,'cols'=8] {'cols'}, dimensions={0}, use_global_device_ids=true | all-gather | bytes 13824 | tf_op jit(solution)/shard_map/all_gather | solution.py:25
  47.3 68.2 %all_gather.17 = f32[512,256]{1,0:T(8,128)S(1)} all-gather(f32[16,256]{1,0:T(8,128)S(1)} %copy-done.2), channel_id=1, replica_groups=mesh['rows'=4,'cols'=8] {'rows','cols'}, dimensions={0}, use_global_device_ids=true | all-gather | bytes 540672 | tf_op jit(solution)/shard_map/all_gather | solution.py:10
  115.6 0.9 fusion.7
  116.5 0.8 fusion.10
  117.4 0.8 copy.42
  119.1 2.3 fusion.11
  121.4 55.9 %reduce-scatter.13.cloned.1.call-done = f32[32,12]{1,0:T(8,128)} async-done(((f32[256,12]{1,0:T(8,128)}), f32[32,12]{1,0:T(8,128)}) %reduce-scatter.13.cloned.1.call-update) | async-done | bytes 1552
  177.3 0.8 copy.43
  178.1 30.5 %all-gather.3 = f32[8,32,12]{1,2,0:T(8,128)S(1)} all-gather(f32[1,32,12]{1,2,0:T(8,128)S(1)} %fusion.9), channel_id=1, replica_groups=mesh['rows'=4,'cols'=8] {'cols'}, dimensions={0}, use_global_device_ids=true | all-gather | bytes 13824 | tf_op jit(solution)/shard_map/all_gather | solution.py:25
  208.7 0.8 copy.45
  209.6 5.2 %all-gather.2 = f32[4,64,32]{1,2,0:T(8,128)S(1)} all-gather(f32[1,64,32]{1,2,0:T(8,128)S(1)} %fusion.8), channel_id=1, replica_groups=mesh['rows'=4,'cols'=8] {'rows'}, dimensions={0}, use_global_device_ids=true | all-gather | bytes 40960 | tf_op jit(solution)/shard_map/all_gather | solution.py:26
  215.0 35.3 %all-reduce.3.cloned.1.call-done = f32[512,256]{1,0:T(8,128)} async-done(((f32[512,256]{1,0:T(8,128)}), f32[512,256]{1,0:T(8,128)}) %all-reduce.3.cloned.1.call-update) | async-done | bytes 524304 | tf_op jit(solution)/shard_map/psum | solution.py:48
  250.3 1.2 multiply_subtract_fusion
  251.5 0.9 fusion.6
  252.4 0.8 fusion.12
  253.2 0.8 copy.46
  255.0 2.2 fusion.13
  257.2 58.0 %reduce-scatter.17.cloned.1.call-done = f32[32,12]{1,0:T(8,128)} async-done(((f32[256,12]{1,0:T(8,128)}), f32[32,12]{1,0:T(8,128)}) %reduce-scatter.17.cloned.1.call-update) | async-done | bytes 1552
  315.2 0.8 copy.47
  316.6 19.6 %reduce-scatter.19.cloned.1.call-done = f32[64,32]{1,0:T(8,128)} async-done(((f32[256,32]{1,0:T(8,128)}), f32[64,32]{1,0:T(8,128)}) %reduce-scatter.19.cloned.1.call-update) | async-done | bytes 8208
  336.2 0.8 copy.49
  337.6 50.6 %all-reduce.5.cloned.1.call-done = f32[512,256]{1,0:T(8,128)} async-done(((f32[512,256]{1,0:T(8,128)}), f32[512,256]{1,0:T(8,128)}) %all-reduce.5.cloned.1.call-update) | async-done | bytes 524304 | tf_op jit(solution)/shard_map/psum | solution.py:48
  388.2 1.3 dynamic-slice_subtract_fusion
  (41 shorter events, 5.1 us)
Async XLA Ops:
  8.0 169.3 %reduce-scatter.13.cloned.1.call-start = ((), (), s32[]{:S(2)}) async-start(), calls=%async_computation.6 | async-start | bytes 147456
  14.5 0.7 copy-start.1
  46.6 0.7 copy-start.2
  46.6 68.9 %copy-start.3 = (f32[12,32,512]{2,1,0:T(8,128)S(1)}, f32[12,32,512]{2,1,0:T(8,128)}, u32[]{:S(2)}) copy-start(f32[12,32,512]{2,1,0:T(8,128)} %param.4) | copy-start | bytes 2359300
  118.2 90.6 %reduce-scatter.15.cloned.1.call-start = ((), (), s32[]{:S(2)}) async-start(), calls=%async_computation.7 | async-start | bytes 163840
  119.0 131.3 %all-reduce.3.cloned.1.call-start = ((), (), s32[]{:S(2)}) async-start(), calls=%async_computation.4 | async-start | bytes 1048576 | tf_op jit(solution)/shard_map/psum | solution.py:48
  121.4 193.8 %reduce-scatter.17.cloned.1.call-start = ((), (), s32[]{:S(2)}) async-start(), calls=%async_computation.8 | async-start | bytes 147456
  208.7 0.8 copy-start
  254.0 82.1 %reduce-scatter.19.cloned.1.call-start = ((), (), s32[]{:S(2)}) async-start(), calls=%async_computation.9 | async-start | bytes 163840
  254.9 133.3 %all-reduce.5.cloned.1.call-start = ((), (), s32[]{:S(2)}) async-start(), calls=%async_computation.5 | async-start | bytes 1048576 | tf_op jit(solution)/shard_map/psum | solution.py:48
Sparse Core Ops, SparseCore 0:
  118.3 58.9 reduce-scatter.12
  179.7 18.6 reduce-scatter.14
  254.2 60.9 reduce-scatter.16
  317.5 18.6 reduce-scatter.18
Sparse Core Ops, SparseCore 1:
  124.8 125.5 all-reduce.2
  260.7 127.5 all-reduce.4
where the time goes:
time: 397 us
  waiting for transfers between devices  219 us (55%)
  blocking collectives  142 us (36%)
  between operations  15.4 us (4%)
  local copies, waits for them, and re-layouts  7.98 us (2%)
  matrix products  7.96 us (2%)
  other arithmetic  3.99 us (1%)
    unnamed x10, waiting for transfers between devices  133 us
    psum x2, waiting for transfers between devices, per_device(): whole_c = whole_c - rate_c * lax.psum(term_c, ('rows', 'cols'))  85.9 us
    all_gather x1, blocking collectives, gather_third(): return lax.all_gather(piece, ('rows', 'cols'), axis=0, tiled=True)  68.2 us
    all_gather x2, blocking collectives, per_device(): whole_a = lax.all_gather(shard_a, 'cols', axis=1, tiled=True)  61.9 us
    all_gather x2, blocking collectives, per_device(): whole_b = lax.all_gather(shard_b, 'rows', axis=1, tiled=True)  11.7 us
  transfers between devices with their start and end apart: 6, of which 5 were waited for; matrix products, arithmetic and copies ran while one was open for 3% of the time, Pallas kernels for 0%

commit v1 on v0

--- a/solution.py
+++ b/solution.py
@@ -1,23 +1,24 @@
+import functools
+
 import jax
 import jax.numpy as jnp
 from jax import lax
+from jax.experimental import pallas as pl
+from jax.experimental.pallas import tpu as pltpu
 from jax.sharding import PartitionSpec as P
 
 STEPS = 2
+MESH = pl.DeviceIdType.MESH
 
 
 def gather_third(piece):
     return lax.all_gather(piece, ("rows", "cols"), axis=0, tiled=True)
 
 
-def per_device(tensor, first_factor, second_factor, third_factor):
+def plain_steps(tensor, first_factor, second_factor, third_factor):
     high = lax.Precision.HIGHEST
     rows_dev, cols_dev, depth = tensor.shape
-    size_i = rows_dev * lax.axis_size("rows")
-    size_j = cols_dev * lax.axis_size("cols")
-    rate_a = 4.0 / jnp.sqrt(jnp.float32(size_j * depth))
-    rate_b = 4.0 / jnp.sqrt(jnp.float32(size_i * depth))
-    rate_c = 4.0 / jnp.sqrt(jnp.float32(size_i * size_j))
+    rate_a, rate_b, rate_c = rates(tensor)
     flat_target = tensor.reshape(-1, depth)
     shard_a, shard_b = (first_factor, second_factor)
     whole_c = gather_third(third_factor)
@@ -33,10 +34,7 @@
         term_a = jnp.einsum("ijr,jr->ir", deriv_c, whole_b, precision=high)
         term_b = jnp.einsum("ijr,ir->jr", deriv_c, whole_a, precision=high)
         term_c = lax.dot_general(
-            deriv,
-            khatri,
-            (((0,), (0,)), ((), ())),
-            precision=high,
+            deriv, khatri, (((0,), (0,)), ((), ())), precision=high,
             preferred_element_type=jnp.float32,
         )
         shard_a = shard_a - rate_a * lax.psum_scatter(
@@ -52,6 +50,244 @@
     return (shard_a, shard_b, shard_c)
 
 
+def rates(tensor):
+    rows_dev, cols_dev, depth = tensor.shape
+    size_i = rows_dev * lax.axis_size("rows")
+    size_j = cols_dev * lax.axis_size("cols")
+    return (
+        4.0 / float(size_j * depth) ** 0.5,
+        4.0 / float(size_i * depth) ** 0.5,
+        4.0 / float(size_i * size_j) ** 0.5,
+    )
+
+
+def split(x):
+    hi = x.astype(jnp.bfloat16)
+    return hi, (x - hi.astype(jnp.float32)).astype(jnp.bfloat16)
+
+
+def dot3(lhs, rhs, dims):
+    def one(a, b):
+        return lax.dot_general(a, b, (dims, ((), ())), preferred_element_type=jnp.float32)
+
+    return one(lhs[0], rhs[0]) + (one(lhs[0], rhs[1]) + one(lhs[1], rhs[0]))
+
+
+def kernel(
+    n_rows, n_cols, rate, target_ref, a_ref, b_ref, c_ref, a_out, b_out, c_out,
+    a_slots, b_slots, c_whole, c_term, from_core, to_x, from_x, to_col, from_col,
+    khatri_hi, khatri_lo, deriv_hi, deriv_lo, place_a, place_b, send_sem, recv_sem,
+):
+    half = n_rows // 2
+    n_i, n_j = a_ref.shape[0], b_ref.shape[0]
+    width_a, width_b = a_ref.shape[1], b_ref.shape[1]
+    rank = c_ref.shape[1]
+    row, col = lax.axis_index("rows"), lax.axis_index("cols")
+    plane, core = lax.div(row, 2), lax.rem(row, 2)
+    other = 1 - core
+    used = []
+
+    def turn(base, offset, size):
+        return lax.rem(base + offset, size)
+
+    def send(src, dst, to_row, to_col_index):
+        number = len(used)
+        copy = pltpu.make_async_remote_copy(
+            src_ref=src, dst_ref=dst, send_sem=send_sem.at[number], recv_sem=recv_sem.at[number],
+            device_id=(to_row, to_col_index), device_id_type=MESH,
+        )
+        used.append(copy)
+        copy.start()
+        return copy
+
+    barrier = pltpu.get_barrier_semaphore()
+    for k in range(1, n_cols):
+        pl.semaphore_signal(barrier, inc=1, device_id=(row, turn(col, k, n_cols)), device_id_type=MESH)
+    for k in range(1, n_rows):
+        pl.semaphore_signal(barrier, inc=1, device_id=(turn(row, k, n_rows), col), device_id_type=MESH)
+    pl.semaphore_wait(barrier, n_cols + n_rows - 2)
+
+    def share_first(version):
+        return [
+            send(a_slots.at[version, col], a_slots.at[version, col], row, turn(col, k, n_cols))
+            for k in range(1, n_cols)
+        ]
+
+    def share_second(version):
+        return [
+            send(b_slots.at[version, row], b_slots.at[version, row], turn(row, k, n_rows), col)
+            for k in range(1, n_rows)
+        ]
+
+    def total(slots, version, copies):
+        for copy in copies:
+            copy.wait_recv()
+        result = slots[version, 0]
+        for k in range(1, slots.shape[1]):
+            result = result + slots[version, k]
+        return result
+
+    def gather_start(version, src):
+        return [
+            send(src, c_whole.at[version, plane, core, col], row, turn(col, k, n_cols))
+            for k in range(1, n_cols)
+        ]
+
+    def gather_finish(version, copies):
+        whole = c_whole.at[version]
+        across, partner = [], []
+        for k in range(n_cols):
+            place = turn(col, n_cols - k, n_cols)
+            if k:
+                copies[k - 1].wait_recv()
+            piece = whole.at[plane, core, place]
+            across.append([
+                send(piece, piece, turn(plane, h, half) * 2 + core, col) for h in range(1, half)
+            ])
+            partner.append(send(piece, piece, plane * 2 + other, col))
+        for k in range(n_cols):
+            place = turn(col, n_cols - k, n_cols)
+            for h in range(1, half):
+                across[k][h - 1].wait_recv()
+                piece = whole.at[turn(plane, half - h, half), core, place]
+                partner.append(send(piece, piece, plane * 2 + other, col))
+        for copy in partner:
+            copy.wait_recv()
+
+    begun = gather_start(0, c_ref)
+    c_whole[0, plane, core, col] = c_ref[...]
+    place_a[...] = jnp.zeros_like(place_a)
+    place_a[:n_i, :width_a] = a_ref[...]
+    a_slots[0, col] = pltpu.roll(place_a[...], col * width_a, 1)
+    place_b[...] = jnp.zeros_like(place_b)
+    place_b[:, :width_b] = b_ref[...]
+    b_slots[0, row] = pltpu.roll(place_b[...], row * width_b, 1)
+    sent_a, sent_b = share_first(0), share_second(0)
+    c_shard = c_ref[...]
+    a_full = total(a_slots, 0, sent_a)
+    b_full = total(b_slots, 0, sent_b)
+
+    for step in range(STEPS):
+        last = step == STEPS - 1
+        for i in range(n_i):
+            rows_here = pl.ds(i * n_j, n_j)
+            hi, lo = split(a_full[i : i + 1, :] * b_full)
+            khatri_hi[rows_here, :] = hi
+            khatri_lo[rows_here, :] = lo
+        gather_finish(step, begun)
+        khatri = khatri_hi[...], khatri_lo[...]
+        c_parts = split(c_whole[step].reshape(-1, rank))
+        model = dot3(khatri, c_parts, ((1,), (1,)))
+        deriv = split(jax.nn.sigmoid(model) - target_ref[...])
+        deriv_hi[...], deriv_lo[...] = deriv
+        term = c_term.at[step]
+        term[...] = dot3(deriv, khatri, ((0,), (0,))).reshape(term.shape)
+        order = [(h, turn(plane, h, half)) for h in list(range(1, half)) + [0]]
+        core_copies = [
+            send(term.at[there, other], from_core.at[step, there], plane * 2 + other, col)
+            for _, there in order
+        ]
+        deriv_c = dot3((deriv_hi[...], deriv_lo[...]), c_parts, ((1,), (0,)))
+        deriv_c = deriv_c.reshape(n_i, n_j, rank)
+        x_copies = []
+        for (h, there), copy in zip(order[:-1], core_copies[:-1]):
+            copy.wait_recv()
+            for k in range(n_cols):
+                place = turn(col, k, n_cols)
+                to_x[step, h - 1, k] = term[there, core, place] + from_core[step, there, place]
+                x_copies.append(
+                    send(to_x.at[step, h - 1, k], from_x.at[step, h - 1, k], there * 2 + core, col)
+                )
+        grad_b = jnp.sum(deriv_c * a_full[:n_i, None, :], axis=0)
+        b_slots[step + 1, row] = grad_b
+        sent_b = share_second(step + 1)
+        grad_a = jnp.sum(deriv_c * b_full[None, :, :], axis=1)
+        a_slots[step + 1, col] = jnp.zeros_like(place_a)
+        a_slots[step + 1, col, :n_i, :] = grad_a
+        sent_a = share_first(step + 1)
+        core_copies[-1].wait_recv()
+        col_copies = []
+        for k in list(range(1, n_cols)) + [0]:
+            place = turn(col, k, n_cols)
+            piece = term[plane, core, place] + from_core[step, plane, place]
+            for h in range(1, half):
+                x_copies[(h - 1) * n_cols + k].wait_recv()
+                piece = piece + from_x[step, h - 1, k]
+            if k:
+                to_col[step, k - 1] = piece
+                col_copies.append(
+                    send(to_col.at[step, k - 1], from_col.at[step, k - 1], row, place)
+                )
+        for k, copy in enumerate(col_copies):
+            copy.wait_recv()
+            piece = piece + from_col[step, k]
+        c_shard = c_shard - rate[2] * piece
+        if not last:
+            c_whole[step + 1, plane, core, col] = c_shard
+            begun = gather_start(step + 1, c_whole.at[step + 1, plane, core, col])
+        else:
+            c_out[...] = c_shard
+        a_full = a_full - rate[0] * total(a_slots, step + 1, sent_a)
+        b_full = b_full - rate[1] * total(b_slots, step + 1, sent_b)
+    back = lax.rem(n_cols - col, n_cols) * width_a
+    a_out[...] = pltpu.roll(a_full, back, 1)[:n_i, :width_a]
+    back = lax.rem(n_rows - row, n_rows) * width_b
+    b_out[...] = pltpu.roll(b_full, back, 1)[:, :width_b]
+    for copy in used:
+        copy.wait_send()
+
+
+def n_copies(n_rows, n_cols):
+    half = n_rows // 2
+    shares = (STEPS + 1) * (n_cols + n_rows - 2)
+    gather = n_cols - 1 + n_cols * (half - 1) + n_cols * half
+    scatter = half + (half - 1) * n_cols + n_cols - 1
+    return shares + STEPS * (gather + scatter)
+
+
+def per_device(tensor, first_factor, second_factor, third_factor):
+    n_rows, n_cols = lax.axis_size("rows"), lax.axis_size("cols")
+    count, rank = third_factor.shape
+    n_i, n_j, depth = tensor.shape
+    if count % 8 or n_rows % 2 or n_j % 16:
+        return plain_steps(tensor, first_factor, second_factor, third_factor)
+    half = n_rows // 2
+    tall = -(-n_i // 8) * 8
+    f32, bf16 = jnp.float32, jnp.bfloat16
+    copies = n_copies(n_rows, n_cols)
+    vmem = pl.BlockSpec(memory_space=pltpu.VMEM)
+    return pl.pallas_call(
+        functools.partial(kernel, n_rows, n_cols, rates(tensor)),
+        out_shape=tuple(
+            jax.ShapeDtypeStruct(x.shape, f32) for x in (first_factor, second_factor, third_factor)
+        ),
+        in_specs=[vmem] * 4,
+        out_specs=(vmem,) * 3,
+        scratch_shapes=[
+            pltpu.VMEM((STEPS + 1, n_cols, tall, rank), f32),
+            pltpu.VMEM((STEPS + 1, n_rows, n_j, rank), f32),
+            pltpu.VMEM((STEPS, half, 2, n_cols, count, rank), f32),
+            pltpu.VMEM((STEPS, half, 2, n_cols, count, rank), f32),
+            pltpu.VMEM((STEPS, half, n_cols, count, rank), f32),
+            pltpu.VMEM((STEPS, max(half - 1, 1), n_cols, count, rank), f32),
+            pltpu.VMEM((STEPS, max(half - 1, 1), n_cols, count, rank), f32),
+            pltpu.VMEM((STEPS, n_cols, count, rank), f32),
+            pltpu.VMEM((STEPS, n_cols, count, rank), f32),
+            pltpu.VMEM((n_i * n_j, rank), bf16),
+            pltpu.VMEM((n_i * n_j, rank), bf16),
+            pltpu.VMEM((n_i * n_j, depth), bf16),
+            pltpu.VMEM((n_i * n_j, depth), bf16),
+            pltpu.VMEM((tall, rank), f32),
+            pltpu.VMEM((n_j, rank), f32),
+            pltpu.SemaphoreType.DMA((copies,)),
+            pltpu.SemaphoreType.DMA((copies,)),
+        ],
+        compiler_params=pltpu.CompilerParams(
+            collective_id=0, has_side_effects=True, vmem_limit_bytes=48 << 20
+        ),
+    )(tensor.reshape(n_i * n_j, depth), first_factor, second_factor, third_factor)
+
+
 def solution(mesh):
     in_specs = (
         P("rows", "cols", None),

time: 397 us -> 56.6 us (0.14)
  waiting for transfers between devices: 219 us -> 0 us
  blocking collectives: 142 us -> 0 us
  Pallas kernels: 0 us -> 50.5 us
  between operations: 15.4 us -> 0.65 us
  matrix products: 7.96 us -> 0 us
  other arithmetic: 3.99 us -> 0 us
    all_gather x5 -> x0, blocking collectives: 142 us -> none  [the longest x1 68.2 us: gather_third(): return lax.all_gather(piece, ('rows', 'cols'), axis=0, tiled=True)]
    unnamed x10 -> x0, waiting for transfers between devices: 133 us -> none
    psum x2 -> x0, waiting for transfers between devices: 85.9 us -> none  [per_device(): whole_c = whole_c - rate_c * lax.psum(term_c, ('rows', 'cols'))]
    pallas_call x0 -> x1, Pallas kernels: none -> 50.5 us  [per_device(): pl.pallas_call(functools.partial(kernel, n_rows, n_cols, rates(tensor)),...]
    dot_general x6 -> x0, matrix products: 7.96 us -> none  [the longest x2 4.52 us: per_device(): lax.dot_general(deriv, khatri, (((0,), (0,)), ((), ())), precision=high,...]
  transfers between devices with their start and end apart: 6 -> 0, of which waited for: 5 -> 0; matrix products, arithmetic and copies ran while one was open for 3% -> 0% of each run, Pallas kernels for 0% -> 0%
where the time goes in v1:
time: 56.6 us; the launch traced here: 56.2 us
  Pallas kernels  50.5 us (89%)
  local copies, waits for them, and re-layouts  5.07 us (9%)
  between operations  0.65 us (1%)
    pallas_call x1, Pallas kernels, per_device(): pl.pallas_call(functools.partial(kernel, n_rows, n_cols, rates(tensor)),...  50.5 us
    unnamed x11, local copies, waits for them, and re-layouts  5.07 us

profile of v1, /device:TPU:0, one launch (start us, length us, event | category | flops | bytes accessed | tf_op | source)
XLA Modules:
  0.0 56.2 jit_solution(14047394739375338798)
XLA Ops:
  0.6 0.0 copy-start
  0.6 1.1 %copy-done = f32[12,32,512]{2,1,0:T(8,128)S(1)} copy-done((f32[12,32,512]{2,1,0:T(8,128)S(1)}, f32[12,32,512]{2,1,0:T(8,128)}, u32[]{:S(2)}) %copy-start) | copy-done | bytes 786456
  1.8 0.0 copy-start.1
  1.8 0.7 %copy-done.1 = f32[32,64]{1,0:T(8,128)S(1)} copy-done((f32[32,64]{1,0:T(8,128)S(1)}, f32[32,64]{1,0:T(8,128)}, u32[]{:S(2)}) %copy-start.1) | copy-done | bytes 8216
  2.5 0.0 copy-start.2
  2.5 0.7 %copy-done.2 = f32[16,256]{1,0:T(8,128)S(1)} copy-done((f32[16,256]{1,0:T(8,128)S(1)}, f32[16,256]{1,0:T(8,128)}, u32[]{:S(2)}) %copy-start.2) | copy-done | bytes 16408
  3.2 0.0 copy-start.3
  3.2 0.7 %copy-done.3 = f32[12,32]{1,0:T(8,128)S(1)} copy-done((f32[12,32]{1,0:T(8,128)S(1)}, f32[12,32]{1,0:T(8,128)}, u32[]{:S(2)}) %copy-start.3) | copy-done | bytes 1560
  3.9 50.5 %shard_map.67 = (f32[12,32]{1,0:T(8,128)S(1)}, f32[32,64]{1,0:T(8,128)S(1)}, f32[16,256]{1,0:T(8,128)S(1)}) custom-call(f32[384,512]{1,0:T(8,128)S(1)} %bitcast.1, f32[12,32]{1,0:T(8,128)S(1)} %copy-done.3, f32[32,64]{1,0:T(8,128)S(1)} %copy-done.1, f32[16,256]{1,0:T(8,128)S(1)} %copy-done.2), custom_call_target="tpu_custom_call" | custom-call | tf_op jit(solution)/shard_map/pallas_call | solution.py:259
  54.4 0.6 %copy.10 = f32[12,32]{1,0:T(8,128)} copy(f32[12,32]{1,0:T(8,128)S(1)} %get-tuple-element.6) | data formatting | bytes 3072
  55.0 0.6 %copy.11 = f32[32,64]{1,0:T(8,128)} copy(f32[32,64]{1,0:T(8,128)S(1)} %get-tuple-element.7) | data formatting | bytes 16384
  55.6 0.6 %copy.12 = f32[16,256]{1,0:T(8,128)} copy(f32[16,256]{1,0:T(8,128)S(1)} %get-tuple-element.8) | data formatting | bytes 32768
Async XLA Ops:
  0.6 1.1 %copy-start = (f32[12,32,512]{2,1,0:T(8,128)S(1)}, f32[12,32,512]{2,1,0:T(8,128)}, u32[]{:S(2)}) copy-start(f32[12,32,512]{2,1,0:T(8,128)} %param.4) | copy-start | bytes 2359300
  1.8 0.7 %copy-start.1 = (f32[32,64]{1,0:T(8,128)S(1)}, f32[32,64]{1,0:T(8,128)}, u32[]{:S(2)}) copy-start(f32[32,64]{1,0:T(8,128)} %b_ref.1) | copy-start | bytes 24580
  2.5 0.7 %copy-start.2 = (f32[16,256]{1,0:T(8,128)S(1)}, f32[16,256]{1,0:T(8,128)}, u32[]{:S(2)}) copy-start(f32[16,256]{1,0:T(8,128)} %c_ref.1) | copy-start | bytes 49156
  3.2 0.7 %copy-start.3 = (f32[12,32]{1,0:T(8,128)S(1)}, f32[12,32]{1,0:T(8,128)}, u32[]{:S(2)}) copy-start(f32[12,32]{1,0:T(8,128)} %a_ref.1) | copy-start | bytes 4612

commit v2 on v0

--- a/solution.py
+++ b/solution.py
@@ -1,23 +1,24 @@
+import functools
+
 import jax
 import jax.numpy as jnp
 from jax import lax
+from jax.experimental import pallas as pl
+from jax.experimental.pallas import tpu as pltpu
 from jax.sharding import PartitionSpec as P
 
 STEPS = 2
+MESH = pl.DeviceIdType.MESH
 
 
 def gather_third(piece):
     return lax.all_gather(piece, ("rows", "cols"), axis=0, tiled=True)
 
 
-def per_device(tensor, first_factor, second_factor, third_factor):
+def plain_steps(tensor, first_factor, second_factor, third_factor):
     high = lax.Precision.HIGHEST
     rows_dev, cols_dev, depth = tensor.shape
-    size_i = rows_dev * lax.axis_size("rows")
-    size_j = cols_dev * lax.axis_size("cols")
-    rate_a = 4.0 / jnp.sqrt(jnp.float32(size_j * depth))
-    rate_b = 4.0 / jnp.sqrt(jnp.float32(size_i * depth))
-    rate_c = 4.0 / jnp.sqrt(jnp.float32(size_i * size_j))
+    rate_a, rate_b, rate_c = rates(tensor)
     flat_target = tensor.reshape(-1, depth)
     shard_a, shard_b = (first_factor, second_factor)
     whole_c = gather_third(third_factor)
@@ -33,10 +34,7 @@
         term_a = jnp.einsum("ijr,jr->ir", deriv_c, whole_b, precision=high)
         term_b = jnp.einsum("ijr,ir->jr", deriv_c, whole_a, precision=high)
         term_c = lax.dot_general(
-            deriv,
-            khatri,
-            (((0,), (0,)), ((), ())),
-            precision=high,
+            deriv, khatri, (((0,), (0,)), ((), ())), precision=high,
             preferred_element_type=jnp.float32,
         )
         shard_a = shard_a - rate_a * lax.psum_scatter(
@@ -50,6 +48,246 @@
     count = third_factor.shape[0]
     shard_c = lax.dynamic_slice_in_dim(whole_c, owner * count, count, 0)
     return (shard_a, shard_b, shard_c)
+
+
+def rates(tensor):
+    rows_dev, cols_dev, depth = tensor.shape
+    size_i = rows_dev * lax.axis_size("rows")
+    size_j = cols_dev * lax.axis_size("cols")
+    return (
+        4.0 / float(size_j * depth) ** 0.5,
+        4.0 / float(size_i * depth) ** 0.5,
+        4.0 / float(size_i * size_j) ** 0.5,
+    )
+
+
+def split(x):
+    hi = x.astype(jnp.bfloat16)
+    return hi, (x - hi.astype(jnp.float32)).astype(jnp.bfloat16)
+
+
+def dot3(lhs, rhs, dims):
+    def one(a, b):
+        return lax.dot_general(a, b, (dims, ((), ())), preferred_element_type=jnp.float32)
+
+    return one(lhs[0], rhs[0]) + (one(lhs[0], rhs[1]) + one(lhs[1], rhs[0]))
+
+
+def kernel(
+    n_rows, n_cols, rate, target_ref, a_ref, b_ref, c_ref, a_out, b_out, c_out,
+    target, a_slots, a_rows, a_leave, a_arrive, b_slots, c_whole, c_leave, c_arrive,
+    khatri_hi, khatri_lo, prob, place_a, place_b, own_sem, send_sem, recv_sem,
+):
+    half = n_rows // 2
+    n_i, n_j = a_ref.shape[0], b_ref.shape[0]
+    width_a, width_b = a_ref.shape[1], b_ref.shape[1]
+    rank = c_ref.shape[1]
+    depth = target.shape[2]
+    row, col = lax.axis_index("rows"), lax.axis_index("cols")
+    plane, core = lax.div(row, 2), lax.rem(row, 2)
+    used = []
+
+    def turn(base, offset, size):
+        return lax.rem(base + offset, size)
+
+    def send(src, dst, to_row, to_col):
+        number = len(used)
+        copy = pltpu.make_async_remote_copy(
+            src_ref=src, dst_ref=dst, send_sem=send_sem.at[number], recv_sem=recv_sem.at[number],
+            device_id=(to_row, to_col), device_id_type=MESH,
+        )
+        used.append(copy)
+        copy.start()
+        return copy
+
+    steps_away = [(h, flip) for h in range(half) for flip in (0, 1)][1:]
+    to_rows = [turn(plane, h, half) * 2 + lax.rem(core + flip, 2) for h, flip in steps_away]
+    of_rows = [turn(plane, half - h, half) * 2 + lax.rem(core + flip, 2) for h, flip in steps_away]
+    to_cols = [turn(col, k, n_cols) for k in range(1, n_cols)]
+
+    own = pltpu.make_async_copy(
+        target_ref.at[:, pl.ds(pl.multiple_of(row * depth, 128), depth)], target.at[row], own_sem.at[0]
+    )
+    own.start()
+    barrier = pltpu.get_barrier_semaphore()
+    for there in to_cols:
+        pl.semaphore_signal(barrier, inc=1, device_id=(row, there), device_id_type=MESH)
+    for there in to_rows:
+        pl.semaphore_signal(barrier, inc=1, device_id=(there, col), device_id_type=MESH)
+    pl.semaphore_wait(barrier, n_cols + n_rows - 2)
+
+    def over_cols(src, dst):
+        return [send(src, dst, row, there) for there in to_cols]
+
+    def over_rows(src, dst):
+        return [send(src, dst, there, col) for there in to_rows]
+
+    def arrived(copies):
+        for copy in copies:
+            copy.wait_recv()
+
+    def total(slots, version):
+        result = slots[version, 0]
+        for k in range(1, slots.shape[1]):
+            result = result + slots[version, k]
+        return result
+
+    def share(slots, version, place, spread):
+        return spread(slots.at[version, place], slots.at[version, place])
+
+    sent_c = over_cols(c_ref, c_whole.at[0, col])
+    place_a[...] = jnp.zeros_like(place_a)
+    place_a[:n_i, :width_a] = a_ref[...]
+    a_slots[0, col] = pltpu.roll(place_a[...], col * width_a, 1)
+    sent_a = share(a_slots, 0, col, over_cols)
+    place_b[...] = jnp.zeros_like(place_b)
+    place_b[:, :width_b] = b_ref[...]
+    b_slots[0, row] = pltpu.roll(place_b[...], row * width_b, 1)
+    sent_b = share(b_slots, 0, row, over_rows)
+    sent_target = [
+        send(
+            target_ref.at[:, pl.ds(pl.multiple_of(there * depth, 128), depth)],
+            target.at[row], there, col,
+        )
+        for there in to_rows
+    ]
+    c_shard = c_ref[...]
+    c_whole[0, col] = c_shard
+    arrived(sent_a)
+    a_own = total(a_slots, 0)
+    a_rows[0, row] = a_own
+    sent_rows = share(a_rows, 0, row, over_rows)
+    arrived(sent_b)
+    b_full = total(b_slots, 0)
+
+    for step in range(STEPS):
+        last = step == STEPS - 1
+        blocks = [row] + of_rows
+        for number, block in enumerate(blocks):
+            if number:
+                sent_rows[number - 1].wait_recv()
+            a_block = a_rows[step, block]
+            for i in range(n_i):
+                hi, lo = split(a_block[i : i + 1, :] * b_full)
+                khatri_hi[block, i * n_j : (i + 1) * n_j, :] = hi
+                khatri_lo[block, i * n_j : (i + 1) * n_j, :] = lo
+            if not number:
+                arrived(sent_c)
+                c_parts = split(c_whole[step].reshape(-1, rank))
+            model = dot3((khatri_hi[block], khatri_lo[block]), c_parts, ((1,), (1,)))
+            prob[block] = jax.nn.sigmoid(model)
+        order = list(range(n_rows)) if step == 0 else list(range(1, n_rows)) + [0]
+        term_c, term_b, term_own = None, None, None
+        sent_terms = [None] * (n_rows - 1)
+        for number in order:
+            block = blocks[number]
+            if step == 0:
+                if number:
+                    sent_target[number - 1].wait_recv()
+                else:
+                    own.wait()
+            deriv = split(prob[block] - target[block])
+            deriv_c = dot3(deriv, c_parts, ((1,), (0,))).reshape(n_i, n_j, rank)
+            term_a = jnp.sum(deriv_c * b_full[None, :, :], axis=1)
+            if number:
+                a_leave[step, number - 1] = jnp.zeros_like(place_a)
+                a_leave[step, number - 1, :n_i, :] = term_a
+                sent_terms[number - 1] = send(
+                    a_leave.at[step, number - 1], a_arrive.at[step, number - 1], block, col
+                )
+            else:
+                term_own = term_a
+            a_block = a_rows[step, block][:n_i, :]
+            part_b = jnp.sum(deriv_c * a_block[:, None, :], axis=0)
+            part_c = dot3(deriv, (khatri_hi[block], khatri_lo[block]), ((0,), (0,)))
+            term_b = part_b if term_b is None else term_b + part_b
+            term_c = part_c if term_c is None else term_c + part_c
+        c_leave[step] = term_c.reshape(c_leave.shape[1:])
+        sent_c = [
+            send(c_leave.at[step, there], c_arrive.at[step, k], row, there)
+            for k, there in enumerate(to_cols)
+        ]
+        b_slots[step + 1, row] = term_b
+        sent_b = share(b_slots, step + 1, row, over_rows)
+        place_a[...] = jnp.zeros_like(place_a)
+        place_a[:n_i, :] = term_own
+        arrived(sent_terms)
+        term_own = place_a[...]
+        for k in range(n_rows - 1):
+            term_own = term_own + a_arrive[step, k]
+        a_slots[step + 1, col] = term_own
+        sent_a = share(a_slots, step + 1, col, over_cols)
+        arrived(sent_c)
+        grad_c = c_leave[step, col]
+        for k in range(n_cols - 1):
+            grad_c = grad_c + c_arrive[step, k]
+        c_shard = c_shard - rate[2] * grad_c
+        if last:
+            c_out[...] = c_shard
+        else:
+            c_whole[step + 1, col] = c_shard
+            sent_c = share(c_whole, step + 1, col, over_cols)
+        arrived(sent_a)
+        a_own = a_own - rate[0] * total(a_slots, step + 1)
+        if not last:
+            a_rows[step + 1, row] = a_own
+            sent_rows = share(a_rows, step + 1, row, over_rows)
+        arrived(sent_b)
+        b_full = b_full - rate[1] * total(b_slots, step + 1)
+    back = lax.rem(n_cols - col, n_cols) * width_a
+    a_out[...] = pltpu.roll(a_own, back, 1)[:n_i, :width_a]
+    back = lax.rem(n_rows - row, n_rows) * width_b
+    b_out[...] = pltpu.roll(b_full, back, 1)[:, :width_b]
+    for copy in used:
+        copy.wait_send()
+
+
+def n_copies(n_rows, n_cols):
+    rows, cols = n_rows - 1, n_cols - 1
+    return rows + (STEPS + 1) * (cols + rows) + STEPS * (rows + cols) + STEPS * (rows + cols)
+
+
+def per_device(tensor, first_factor, second_factor, third_factor):
+    n_rows, n_cols = lax.axis_size("rows"), lax.axis_size("cols")
+    count, rank = third_factor.shape
+    n_i, n_j, depth = tensor.shape
+    part = depth // n_rows
+    if count % 8 or n_rows % 2 or n_j % 16 or part % 128:
+        return plain_steps(tensor, first_factor, second_factor, third_factor)
+    tall = -(-n_i // 8) * 8
+    f32, bf16 = jnp.float32, jnp.bfloat16
+    copies = n_copies(n_rows, n_cols)
+    vmem = pl.BlockSpec(memory_space=pltpu.VMEM)
+    return pl.pallas_call(
+        functools.partial(kernel, n_rows, n_cols, rates(tensor)),
+        out_shape=tuple(
+            jax.ShapeDtypeStruct(x.shape, f32) for x in (first_factor, second_factor, third_factor)
+        ),
+        in_specs=[pl.BlockSpec(memory_space=pltpu.HBM)] + [vmem] * 3,
+        out_specs=(vmem,) * 3,
+        scratch_shapes=[
+            pltpu.VMEM((n_rows, n_i * n_j, part), f32),
+            pltpu.VMEM((STEPS + 1, n_cols, tall, rank), f32),
+            pltpu.VMEM((STEPS, n_rows, tall, rank), f32),
+            pltpu.VMEM((STEPS, n_rows - 1, tall, rank), f32),
+            pltpu.VMEM((STEPS, n_rows - 1, tall, rank), f32),
+            pltpu.VMEM((STEPS + 1, n_rows, n_j, rank), f32),
+            pltpu.VMEM((STEPS, n_cols, count, rank), f32),
+            pltpu.VMEM((STEPS, n_cols, count, rank), f32),
+            pltpu.VMEM((STEPS, n_cols - 1, count, rank), f32),
+            pltpu.VMEM((n_rows, n_i * n_j, rank), bf16),
+            pltpu.VMEM((n_rows, n_i * n_j, rank), bf16),
+            pltpu.VMEM((n_rows, n_i * n_j, part), f32),
+            pltpu.VMEM((tall, rank), f32),
+            pltpu.VMEM((n_j, rank), f32),
+            pltpu.SemaphoreType.DMA((1,)),
+            pltpu.SemaphoreType.DMA((copies,)),
+            pltpu.SemaphoreType.DMA((copies,)),
+        ],
+        compiler_params=pltpu.CompilerParams(
+            collective_id=0, has_side_effects=True, vmem_limit_bytes=48 << 20
+        ),
+    )(tensor.reshape(n_i * n_j, depth), first_factor, second_factor, third_factor)
 
 
 def solution(mesh):

time: 397 us -> 50.2 us (0.13)
  waiting for transfers between devices: 219 us -> 0 us
  blocking collectives: 142 us -> 0 us
  Pallas kernels: 0 us -> 44.1 us
  between operations: 15.4 us -> 0.65 us
  matrix products: 7.96 us -> 0 us
  other arithmetic: 3.99 us -> 0 us
    all_gather x5 -> x0, blocking collectives: 142 us -> none  [the longest x1 68.2 us: gather_third(): return lax.all_gather(piece, ('rows', 'cols'), axis=0, tiled=True)]
    unnamed x10 -> x0, waiting for transfers between devices: 133 us -> none
    psum x2 -> x0, waiting for transfers between devices: 85.9 us -> none  [per_device(): whole_c = whole_c - rate_c * lax.psum(term_c, ('rows', 'cols'))]
    pallas_call x0 -> x1, Pallas kernels: none -> 44.1 us  [per_device(): pl.pallas_call(functools.partial(kernel, n_rows, n_cols, rates(tensor)),...]
    dot_general x6 -> x0, matrix products: 7.96 us -> none  [the longest x2 4.52 us: per_device(): lax.dot_general(deriv, khatri, (((0,), (0,)), ((), ())), precision=high,...]
  transfers between devices with their start and end apart: 6 -> 0, of which waited for: 5 -> 0; matrix products, arithmetic and copies ran while one was open for 3% -> 0% of each run, Pallas kernels for 0% -> 0%
where the time goes in v2:
time: 50.2 us; the launch traced here: 49.8 us
  Pallas kernels  44.1 us (88%)
  local copies, waits for them, and re-layouts  5.07 us (10%)
  between operations  0.65 us (1%)
    pallas_call x1, Pallas kernels, per_device(): pl.pallas_call(functools.partial(kernel, n_rows, n_cols, rates(tensor)),...  44.1 us
    unnamed x11, local copies, waits for them, and re-layouts  5.07 us

profile of v2, /device:TPU:0, one launch (start us, length us, event | category | flops | bytes accessed | tf_op | source)
XLA Modules:
  0.0 49.8 jit_solution(2853500753537812630)
XLA Ops:
  0.6 0.0 copy-start
  0.6 1.1 %copy-done = f32[12,32,512]{2,1,0:T(8,128)S(1)} copy-done((f32[12,32,512]{2,1,0:T(8,128)S(1)}, f32[12,32,512]{2,1,0:T(8,128)}, u32[]{:S(2)}) %copy-start) | copy-done | bytes 786456
  1.8 0.0 copy-start.1
  1.8 0.7 %copy-done.1 = f32[32,64]{1,0:T(8,128)S(1)} copy-done((f32[32,64]{1,0:T(8,128)S(1)}, f32[32,64]{1,0:T(8,128)}, u32[]{:S(2)}) %copy-start.1) | copy-done | bytes 8216
  2.5 0.0 copy-start.2
  2.5 0.7 %copy-done.2 = f32[16,256]{1,0:T(8,128)S(1)} copy-done((f32[16,256]{1,0:T(8,128)S(1)}, f32[16,256]{1,0:T(8,128)}, u32[]{:S(2)}) %copy-start.2) | copy-done | bytes 16408
  3.2 0.0 copy-start.3
  3.2 0.7 %copy-done.3 = f32[12,32]{1,0:T(8,128)S(1)} copy-done((f32[12,32]{1,0:T(8,128)S(1)}, f32[12,32]{1,0:T(8,128)}, u32[]{:S(2)}) %copy-start.3) | copy-done | bytes 1560
  3.9 44.1 %shard_map.67 = (f32[12,32]{1,0:T(8,128)S(1)}, f32[32,64]{1,0:T(8,128)S(1)}, f32[16,256]{1,0:T(8,128)S(1)}) custom-call(f32[384,512]{1,0:T(8,128)S(1)} %bitcast.1, f32[12,32]{1,0:T(8,128)S(1)} %copy-done.3, f32[32,64]{1,0:T(8,128)S(1)} %copy-done.1, f32[16,256]{1,0:T(8,128)S(1)} %copy-done.2), custom_call_target="tpu_custom_call" | custom-call | tf_op jit(solution)/shard_map/pallas_call | solution.py:261
  48.0 0.6 %copy.10 = f32[12,32]{1,0:T(8,128)} copy(f32[12,32]{1,0:T(8,128)S(1)} %get-tuple-element.6) | data formatting | bytes 3072
  48.6 0.6 %copy.11 = f32[32,64]{1,0:T(8,128)} copy(f32[32,64]{1,0:T(8,128)S(1)} %get-tuple-element.7) | data formatting | bytes 16384
  49.2 0.6 %copy.12 = f32[16,256]{1,0:T(8,128)} copy(f32[16,256]{1,0:T(8,128)S(1)} %get-tuple-element.8) | data formatting | bytes 32768
Async XLA Ops:
  0.6 1.1 %copy-start = (f32[12,32,512]{2,1,0:T(8,128)S(1)}, f32[12,32,512]{2,1,0:T(8,128)}, u32[]{:S(2)}) copy-start(f32[12,32,512]{2,1,0:T(8,128)} %param.4) | copy-start | bytes 2359300
  1.8 0.7 %copy-start.1 = (f32[32,64]{1,0:T(8,128)S(1)}, f32[32,64]{1,0:T(8,128)}, u32[]{:S(2)}) copy-start(f32[32,64]{1,0:T(8,128)} %b_ref.1) | copy-start | bytes 24580
  2.5 0.7 %copy-start.2 = (f32[16,256]{1,0:T(8,128)S(1)}, f32[16,256]{1,0:T(8,128)}, u32[]{:S(2)}) copy-start(f32[16,256]{1,0:T(8,128)} %c_ref.1) | copy-start | bytes 49156
  3.2 0.7 %copy-start.3 = (f32[12,32]{1,0:T(8,128)S(1)}, f32[12,32]{1,0:T(8,128)}, u32[]{:S(2)}) copy-start(f32[12,32]{1,0:T(8,128)} %a_ref.1) | copy-start | bytes 4612

commit v3 on v2

--- a/solution.py
+++ b/solution.py
@@ -179,6 +179,7 @@
         order = list(range(n_rows)) if step == 0 else list(range(1, n_rows)) + [0]
         term_c, term_b, term_own = None, None, None
         sent_terms = [None] * (n_rows - 1)
+        derivs = {}
         for number in order:
             block = blocks[number]
             if step == 0:
@@ -186,8 +187,17 @@
                     sent_target[number - 1].wait_recv()
                 else:
                     own.wait()
-            deriv = split(prob[block] - target[block])
-            deriv_c = dot3(deriv, c_parts, ((1,), (0,))).reshape(n_i, n_j, rank)
+            derivs[number] = split(prob[block] - target[block])
+            part_c = dot3(derivs[number], (khatri_hi[block], khatri_lo[block]), ((0,), (0,)))
+            term_c = part_c if term_c is None else term_c + part_c
+        c_leave[step] = term_c.reshape(c_leave.shape[1:])
+        sent_c = [
+            send(c_leave.at[step, there], c_arrive.at[step, k], row, there)
+            for k, there in enumerate(to_cols)
+        ]
+        for number in list(range(1, n_rows)) + [0]:
+            block = blocks[number]
+            deriv_c = dot3(derivs[number], c_parts, ((1,), (0,))).reshape(n_i, n_j, rank)
             term_a = jnp.sum(deriv_c * b_full[None, :, :], axis=1)
             if number:
                 a_leave[step, number - 1] = jnp.zeros_like(place_a)
@@ -199,14 +209,7 @@
                 term_own = term_a
             a_block = a_rows[step, block][:n_i, :]
             part_b = jnp.sum(deriv_c * a_block[:, None, :], axis=0)
-            part_c = dot3(deriv, (khatri_hi[block], khatri_lo[block]), ((0,), (0,)))
             term_b = part_b if term_b is None else term_b + part_b
-            term_c = part_c if term_c is None else term_c + part_c
-        c_leave[step] = term_c.reshape(c_leave.shape[1:])
-        sent_c = [
-            send(c_leave.at[step, there], c_arrive.at[step, k], row, there)
-            for k, there in enumerate(to_cols)
-        ]
         b_slots[step + 1, row] = term_b
         sent_b = share(b_slots, step + 1, row, over_rows)
         place_a[...] = jnp.zeros_like(place_a)

time: 50.2 us -> 49.7 us (0.990)
    pallas_call x1, Pallas kernels: 44.1 us -> 43.6 us  [per_device(): pl.pallas_call(functools.partial(kernel, n_rows, n_cols, rates(tensor)),...]
where the time goes in v3:
time: 49.7 us; the launch traced here: 49.3 us
  Pallas kernels  43.6 us (88%)
  local copies, waits for them, and re-layouts  5.07 us (10%)
  between operations  0.65 us (1%)
    pallas_call x1, Pallas kernels, per_device(): pl.pallas_call(functools.partial(kernel, n_rows, n_cols, rates(tensor)),...  43.6 us
    unnamed x11, local copies, waits for them, and re-layouts  5.07 us

profile of v3, /device:TPU:0, one launch (start us, length us, event | category | flops | bytes accessed | tf_op | source)
XLA Modules:
  0.0 49.3 jit_solution(5897068548290422773)
XLA Ops:
  0.6 0.0 copy-start
  0.6 1.1 %copy-done = f32[12,32,512]{2,1,0:T(8,128)S(1)} copy-done((f32[12,32,512]{2,1,0:T(8,128)S(1)}, f32[12,32,512]{2,1,0:T(8,128)}, u32[]{:S(2)}) %copy-start) | copy-done | bytes 786456
  1.8 0.0 copy-start.1
  1.8 0.7 %copy-done.1 = f32[32,64]{1,0:T(8,128)S(1)} copy-done((f32[32,64]{1,0:T(8,128)S(1)}, f32[32,64]{1,0:T(8,128)}, u32[]{:S(2)}) %copy-start.1) | copy-done | bytes 8216
  2.5 0.0 copy-start.2
  2.5 0.7 %copy-done.2 = f32[16,256]{1,0:T(8,128)S(1)} copy-done((f32[16,256]{1,0:T(8,128)S(1)}, f32[16,256]{1,0:T(8,128)}, u32[]{:S(2)}) %copy-start.2) | copy-done | bytes 16408
  3.2 0.0 copy-start.3
  3.2 0.7 %copy-done.3 = f32[12,32]{1,0:T(8,128)S(1)} copy-done((f32[12,32]{1,0:T(8,128)S(1)}, f32[12,32]{1,0:T(8,128)}, u32[]{:S(2)}) %copy-start.3) | copy-done | bytes 1560
  3.9 43.6 %shard_map.67 = (f32[12,32]{1,0:T(8,128)S(1)}, f32[32,64]{1,0:T(8,128)S(1)}, f32[16,256]{1,0:T(8,128)S(1)}) custom-call(f32[384,512]{1,0:T(8,128)S(1)} %bitcast.1, f32[12,32]{1,0:T(8,128)S(1)} %copy-done.3, f32[32,64]{1,0:T(8,128)S(1)} %copy-done.1, f32[16,256]{1,0:T(8,128)S(1)} %copy-done.2), custom_call_target="tpu_custom_call" | custom-call | tf_op jit(solution)/shard_map/pallas_call | solution.py:264
  47.5 0.6 %copy.10 = f32[12,32]{1,0:T(8,128)} copy(f32[12,32]{1,0:T(8,128)S(1)} %get-tuple-element.6) | data formatting | bytes 3072
  48.1 0.6 %copy.11 = f32[32,64]{1,0:T(8,128)} copy(f32[32,64]{1,0:T(8,128)S(1)} %get-tuple-element.7) | data formatting | bytes 16384
  48.7 0.6 %copy.12 = f32[16,256]{1,0:T(8,128)} copy(f32[16,256]{1,0:T(8,128)S(1)} %get-tuple-element.8) | data formatting | bytes 32768
Async XLA Ops:
  0.6 1.1 %copy-start = (f32[12,32,512]{2,1,0:T(8,128)S(1)}, f32[12,32,512]{2,1,0:T(8,128)}, u32[]{:S(2)}) copy-start(f32[12,32,512]{2,1,0:T(8,128)} %param.4) | copy-start | bytes 2359300
  1.8 0.7 %copy-start.1 = (f32[32,64]{1,0:T(8,128)S(1)}, f32[32,64]{1,0:T(8,128)}, u32[]{:S(2)}) copy-start(f32[32,64]{1,0:T(8,128)} %b_ref.1) | copy-start | bytes 24580
  2.5 0.7 %copy-start.2 = (f32[16,256]{1,0:T(8,128)S(1)}, f32[16,256]{1,0:T(8,128)}, u32[]{:S(2)}) copy-start(f32[16,256]{1,0:T(8,128)} %c_ref.1) | copy-start | bytes 49156
  3.2 0.7 %copy-start.3 = (f32[12,32]{1,0:T(8,128)S(1)}, f32[12,32]{1,0:T(8,128)}, u32[]{:S(2)}) copy-start(f32[12,32]{1,0:T(8,128)} %a_ref.1) | copy-start | bytes 4612
